TPU v7x, 32 devices: a whole 2x2x4 slice. The times are simulated.
32 devices in a mesh: row: 8 (over z, core), col: 4 (over y, x).
Axes of the slice: x: 2, y: 2, z: 4, core: 2. Of those that a mesh axis runs over, the one named last changes fastest.
Arguments:
- points: bfloat16 [2048, 1024], P(('row', 'col')), may hold values from -6 to 6
- factor: float32 [2048, 256], P(('row', 'col')), may hold values from 0 to 1
Outputs:
- factor_out: float32 [2048, 256], P(('row', 'col'))
All inputs are finite; a program needn't handle non-finite values.
Results may differ from a plain program's by a relative error of at most 0.002.
The roundings to bfloat16 on the way count: a program that leaves them out, or rounds other values in their place, can miss the bound.
Values may be sent and summed in bfloat16 or wider, within the bound.
A program may use at most 64 MiB of HBM per device.

v0:
```python
import math
import jax
import jax.numpy as jnp
from jax import lax
from jax.sharding import PartitionSpec as P

EMBED_WIDTH = 1024
ITERS = 2


def shards(points, factor):
    nrow = lax.axis_size("row")
    ncol = lax.axis_size("col")
    pts = points.shape[0]
    rank = factor.shape[1]
    total = pts * nrow * ncol
    row_pts = lax.all_gather(points, "col", axis=0, tiled=True)
    col_pts = lax.all_gather(points, "row", axis=0, tiled=True)
    gram_matrix = lax.dot_general(
        row_pts, col_pts, (((1,), (1,)), ((), ())), preferred_element_type=jnp.float32
    )
    row_sq = jnp.sum(jnp.square(row_pts.astype(jnp.float32)), axis=1)
    col_sq = jnp.sum(jnp.square(col_pts.astype(jnp.float32)), axis=1)
    kern = jnp.exp((2.0 * gram_matrix - row_sq[:, None] - col_sq[None, :]) * (0.5 / EMBED_WIDTH))
    row_sum, band = lax.psum((jnp.sum(kern, axis=1), jnp.sum(kern)), "col")
    col_sum, grand = lax.psum((jnp.sum(kern, axis=0), band), "row")
    affinity = (
        kern - row_sum[:, None] / total - col_sum[None, :] / total + grand / (total * total)
    ).astype(jnp.bfloat16)
    unit = 2.0 / math.sqrt(total * rank)
    h = factor * unit
    for step in range(ITERS):
        hb = h.astype(jnp.bfloat16)
        copies = lax.all_gather(hb, "row", axis=0, tiled=True)
        ah = lax.psum_scatter(
            jnp.dot(affinity, copies, preferred_element_type=jnp.float32),
            "col",
            scatter_dimension=0,
            tiled=True,
        )
        local_gram = lax.dot_general(
            h, h, (((0,), (0,)), ((), ())), precision=lax.Precision.HIGHEST
        )
        hh = lax.psum(local_gram, ("row", "col"))
        scale = 0.5 / jnp.sqrt(jnp.sum(hh * hh) + 1e-06)
        h = jnp.maximum(h - scale * (jnp.dot(h, hh, precision=lax.Precision.HIGHEST) - ah), 0.0)
    return h / unit


def solution(mesh):
    in_specs = (P(("row", "col"), None), P(("row", "col"), None))
    out_specs = P(("row", "col"), None)
    return jax.shard_map(shards, mesh=mesh, in_specs=in_specs, out_specs=out_specs, check_vma=False)
```

profile of v0, /device:TPU:0, one launch (start us, length us, event | category | flops | bytes accessed | tf_op | source)
XLA Modules:
  0.0 301.0 jit_solution(7194826416192646812)
XLA Ops:
  7.4 0.0 copy-start.1
  7.4 0.0 all-gather.2.cloned.1.call-start
  7.4 0.7 all-gather.2.cloned.1.call-update
  8.1 0.0 all-reduce.5.cloned.1.call-start
  8.1 2.0 fusion.12
  10.2 0.0 all-reduce.5.cloned.1.call-update
  10.2 0.0 reduce-scatter.3.cloned.1.call-start
  10.3 11.9 %all_gather.12 = bf16[256,1024]{1,0:T(8,128)(2,1)S(1)} all-gather(bf16[64,1024]{1,0:T(8,128)(2,1)} %param.2), channel_id=1, replica_groups=mesh['row'=8,'col'=4] {'col'}, dimensions={0}, use_global_device_ids=true | all-gather | bytes 655360 | tf_op jit(solution)/shard_map/all_gather | solution.py:17
  22.1 0.0 copy-done.1
  22.2 0.2 multiply_reduce_fusion.1
  22.3 15.2 %all_gather.14 = bf16[512,256]{1,0:T(8,128)(2,1)S(1)} all-gather(bf16[64,256]{1,0:T(8,128)(2,1)S(1)} %multiply_convert_fusion), channel_id=1, replica_groups=mesh['row'=8,'col'=4] {'row'}, dimensions={0}, use_global_device_ids=true | all-gather | bytes 294912 | tf_op jit(solution)/shard_map/all_gather | solution.py:34
  37.6 0.0 all-gather.2.cloned.1.call-done
  37.6 0.0 copy-start
  37.6 1.6 multiply_reduce_fusion
  39.2 0.0 copy-done
  39.2 1.2 fusion.20
  40.4 9.6 %all-reduce.1 = (f32[]{:T(128)}, f32[256]{0:T(256)S(1)}) all-reduce(f32[]{:T(128)} %get-tuple-element.6, f32[256]{0:T(256)S(1)} %get-tuple-element.5), channel_id=1, replica_groups=mesh['row'=8,'col'=4] {'col'}, use_global_device_ids=true, to_apply=%region_9.0 | all-reduce | flops 257 | bytes 2056 | tf_op jit(solution)/shard_map/psum | solution.py:25
  50.0 15.4 %all-reduce = (f32[]{:T(128)}, f32[512]{0:T(512)S(1)}) all-reduce(f32[]{:T(128)} %get-tuple-element.10, f32[512]{0:T(512)S(1)} %get-tuple-element.7), channel_id=1, replica_groups=mesh['row'=8,'col'=4] {'row'}, use_global_device_ids=true, to_apply=%region_10.0 | all-reduce | flops 513 | bytes 4104 | tf_op jit(solution)/shard_map/psum | solution.py:26
  66.1 1.0 fusion.19
  67.1 0.0 reduce-scatter.3.cloned.1.call-update
  67.1 0.0 all-reduce.7.cloned.1.call-start
  67.2 78.5 %all-reduce.5.cloned.1.call-done = f32[256,256]{1,0:T(8,128)} async-done(((f32[256,256]{1,0:T(8,128)}), f32[256,256]{1,0:T(8,128)}) %all-reduce.5.cloned.1.call-update) | async-done | bytes 262160 | tf_op jit(solution)/shard_map/psum | solution.py:44
  145.6 1.6 multiply_reduce_fusion.3
  147.9 0.0 reduce-scatter.3.cloned.1.call-done
  148.0 1.2 fusion.21
  149.2 14.2 %all_gather.15 = bf16[512,256]{1,0:T(8,128)(2,1)S(1)} all-gather(bf16[64,256]{1,0:T(8,128)(2,1)S(1)} %get-tuple-element.13), channel_id=1, replica_groups=mesh['row'=8,'col'=4] {'row'}, dimensions={0}, use_global_device_ids=true | all-gather | bytes 294912 | tf_op jit(solution)/shard_map/all_gather | solution.py:34
  163.4 1.1 fusion.22
  164.5 0.0 all-reduce.7.cloned.1.call-update
  164.5 0.0 reduce-scatter.5.cloned.1.call-start
  164.6 1.0 fusion.18
  165.6 0.0 reduce-scatter.5.cloned.1.call-update
  165.6 124.1 %all-reduce.7.cloned.1.call-done = f32[256,256]{1,0:T(8,128)} async-done(((f32[256,256]{1,0:T(8,128)}), f32[256,256]{1,0:T(8,128)}) %all-reduce.7.cloned.1.call-update) | async-done | bytes 262160 | tf_op jit(solution)/shard_map/psum | solution.py:44
  289.7 1.6 multiply_reduce_fusion.2
  292.0 0.0 reduce-scatter.5.cloned.1.call-done
  292.0 1.8 fusion.7
  (3 shorter events, 0.0 us)
Async XLA Ops:
  7.4 14.8 %copy-start.1 = (f32[64,256]{1,0:T(8,128)S(1)}, f32[64,256]{1,0:T(8,128)}, u32[]{:S(2)}) copy-start(f32[64,256]{1,0:T(8,128)} %param.3) | copy-start | bytes 196612
  7.4 30.2 %all-gather.2.cloned.1.call-start = ((), (), s32[]{:S(2)}) async-start(), calls=%async_computation.3 | async-start | bytes 1179648 | tf_op jit(solution)/shard_map/all_gather | solution.py:18
  8.1 137.5 %all-reduce.5.cloned.1.call-start = ((), (), s32[]{:S(2)}) async-start(), calls=%async_computation.2 | async-start | bytes 524288 | tf_op jit(solution)/shard_map/psum | solution.py:44
  10.2 137.8 %reduce-scatter.3.cloned.1.call-start = ((), (), s32[]{:S(2)}) async-start(), calls=%async_computation.4 | async-start | bytes 327680 | tf_op jit(solution)/shard_map/reduce_scatter | solution.py:35
  37.6 1.6 copy-start
  67.1 222.6 %all-reduce.7.cloned.1.call-start = ((), (), s32[]{:S(2)}) async-start(), calls=%async_computation.5 | async-start | bytes 524288 | tf_op jit(solution)/shard_map/psum | solution.py:44
  164.5 127.5 %reduce-scatter.5.cloned.1.call-start = ((), (), s32[]{:S(2)}) async-start(), calls=%async_computation.6 | async-start | bytes 327680 | tf_op jit(solution)/shard_map/reduce_scatter | solution.py:35
Sparse Core Ops, SparseCore 0:
  9.8 26.2 all-gather.1
  67.2 21.1 reduce-scatter.2
  168.1 23.4 reduce-scatter.4
Sparse Core Ops, SparseCore 1:
  14.1 131.5 all-reduce.4
  164.6 125.0 all-reduce.6
where the time goes:
time: 301 us
  waiting for transfers between devices  203 us (67%)
  blocking collectives  66.4 us (22%)
  between operations  16.6 us (6%)
  matrix products  9.4 us (3%)
  other arithmetic  5.03 us (2%)
    psum x2, waiting for transfers between devices, shards(): hh = lax.psum(local_gram, ('row', 'col'))  203 us
    all_gather x2, blocking collectives, shards(): copies = lax.all_gather(hb, 'row', axis=0, tiled=True)  29.4 us
    psum x1, blocking collectives, shards(): col_sum, grand = lax.psum((jnp.sum(kern, axis=0), band), 'row')  15.4 us
    all_gather x1, blocking collectives, shards(): row_pts = lax.all_gather(points, 'col', axis=0, tiled=True)  11.9 us
    psum x1, blocking collectives, shards(): row_sum, band = lax.psum((jnp.sum(kern, axis=1), jnp.sum(kern)), 'col')  9.6 us
  transfers between devices with their start and end apart: 5, of which 2 were waited for; matrix products, arithmetic and copies ran while one was open for 3% of the time, Pallas kernels for 0%

commit v1 on v0

--- a/solution.py
+++ b/solution.py
@@ -41,7 +41,7 @@
         local_gram = lax.dot_general(
             h, h, (((0,), (0,)), ((), ())), precision=lax.Precision.HIGHEST
         )
-        hh = lax.psum(local_gram, ("row", "col"))
+        hh = lax.psum(lax.psum(local_gram, "col"), "row")
         scale = 0.5 / jnp.sqrt(jnp.sum(hh * hh) + 1e-06)
         h = jnp.maximum(h - scale * (jnp.dot(h, hh, precision=lax.Precision.HIGHEST) - ah), 0.0)
     return h / unit

time: 301 us -> 227 us (0.75)
  waiting for transfers between devices: 203 us -> 129 us
    psum x2 -> x4, waiting for transfers between devices: 203 us -> 128 us  [shards(): hh = lax.psum(lax.psum(local_gram, 'col'), 'row')]
  transfers between devices with their start and end apart: 5 -> 7, of which waited for: 2 -> 4; matrix products, arithmetic and copies ran while one was open for 3% -> 4% of each run, Pallas kernels for 0% -> 0%
where the time goes in v1:
time: 227 us
  waiting for transfers between devices  129 us (57%)
  blocking collectives  66.6 us (29%)
  between operations  16.9 us (7%)
  matrix products  9.44 us (4%)
  other arithmetic  5.03 us (2%)
    psum x4, waiting for transfers between devices, shards(): hh = lax.psum(lax.psum(local_gram, 'col'), 'row')  128 us
    all_gather x2, blocking collectives, shards(): copies = lax.all_gather(hb, 'row', axis=0, tiled=True)  29.4 us
    psum x1, blocking collectives, shards(): col_sum, grand = lax.psum((jnp.sum(kern, axis=0), band), 'row')  14.5 us
    all_gather x1, blocking collectives, shards(): row_pts = lax.all_gather(points, 'col', axis=0, tiled=True)  13.2 us
    psum x1, blocking collectives, shards(): row_sum, band = lax.psum((jnp.sum(kern, axis=1), jnp.sum(kern)), 'col')  9.53 us
  transfers between devices with their start and end apart: 7, of which 4 were waited for; matrix products, arithmetic and copies ran while one was open for 4% of the time, Pallas kernels for 0%

profile of v1, /device:TPU:0, one launch (start us, length us, event | category | flops | bytes accessed | tf_op | source)
XLA Modules:
  0.0 226.8 jit_solution(3958368545448687593)
XLA Ops:
  7.4 0.0 copy-start.1
  7.4 0.0 all-reduce.7.cloned.1.call-start
  7.4 2.1 fusion.12
  9.4 0.0 all-reduce.7.cloned.1.call-update
  9.5 0.0 all-gather.2.cloned.1.call-start
  9.5 0.5 all-gather.2.cloned.1.call-update
  10.1 0.0 all-reduce.9.cloned.1.call-start
  10.1 13.2 %all_gather.12 = bf16[256,1024]{1,0:T(8,128)(2,1)S(1)} all-gather(bf16[64,1024]{1,0:T(8,128)(2,1)} %param.2), channel_id=1, replica_groups=mesh['row'=8,'col'=4] {'col'}, dimensions={0}, use_global_device_ids=true | all-gather | bytes 655360 | tf_op jit(solution)/shard_map/all_gather | solution.py:17
  23.3 0.0 copy-done.1
  23.3 15.2 %all_gather.14 = bf16[512,256]{1,0:T(8,128)(2,1)S(1)} all-gather(bf16[64,256]{1,0:T(8,128)(2,1)S(1)} %multiply_convert_fusion), channel_id=1, replica_groups=mesh['row'=8,'col'=4] {'row'}, dimensions={0}, use_global_device_ids=true | all-gather | bytes 294912 | tf_op jit(solution)/shard_map/all_gather | solution.py:34
  38.6 0.2 multiply_reduce_fusion.1
  38.7 18.9 %all-reduce.7.cloned.1.call-done = f32[256,256]{1,0:T(8,128)} async-done(((f32[256,256]{1,0:T(8,128)}), f32[256,256]{1,0:T(8,128)}) %all-reduce.7.cloned.1.call-update) | async-done | bytes 262160 | tf_op jit(solution)/shard_map/psum | solution.py:44
  57.6 0.0 all-reduce.9.cloned.1.call-update
  57.6 0.0 reduce-scatter.3.cloned.1.call-start
  57.7 0.0 all-gather.2.cloned.1.call-done
  57.7 0.0 copy-start
  57.7 1.6 multiply_reduce_fusion
  59.3 0.0 copy-done
  59.3 1.2 fusion.20
  60.6 9.5 %all-reduce.1 = (f32[]{:T(128)}, f32[256]{0:T(256)S(1)}) all-reduce(f32[]{:T(128)} %get-tuple-element.6, f32[256]{0:T(256)S(1)} %get-tuple-element.5), channel_id=1, replica_groups=mesh['row'=8,'col'=4] {'col'}, use_global_device_ids=true, to_apply=%region_10.0 | all-reduce | flops 257 | bytes 2056 | tf_op jit(solution)/shard_map/psum | solution.py:25
  70.1 14.5 %all-reduce = (f32[]{:T(128)}, f32[512]{0:T(512)S(1)}) all-reduce(f32[]{:T(128)} %get-tuple-element.10, f32[512]{0:T(512)S(1)} %get-tuple-element.7), channel_id=1, replica_groups=mesh['row'=8,'col'=4] {'row'}, use_global_device_ids=true, to_apply=%region_11.0 | all-reduce | flops 513 | bytes 4104 | tf_op jit(solution)/shard_map/psum | solution.py:26
  85.2 1.0 fusion.19
  86.2 0.0 reduce-scatter.3.cloned.1.call-update
  86.3 0.0 all-reduce.11.cloned.1.call-start
  86.3 26.7 %all-reduce.9.cloned.1.call-done = f32[256,256]{1,0:T(8,128)} async-done(((f32[256,256]{1,0:T(8,128)}), f32[256,256]{1,0:T(8,128)}) %all-reduce.9.cloned.1.call-update) | async-done | bytes 262160 | tf_op jit(solution)/shard_map/psum | solution.py:44
  113.0 1.6 multiply_reduce_fusion.3
  115.3 0.0 reduce-scatter.3.cloned.1.call-done
  115.3 1.2 fusion.21
  116.5 1.1 fusion.22
  117.6 0.0 all-reduce.11.cloned.1.call-update
  117.7 0.0 all-reduce.13.cloned.1.call-start
  117.7 14.2 %all_gather.15 = bf16[512,256]{1,0:T(8,128)(2,1)S(1)} all-gather(bf16[64,256]{1,0:T(8,128)(2,1)S(1)} %get-tuple-element.13), channel_id=1, replica_groups=mesh['row'=8,'col'=4] {'row'}, dimensions={0}, use_global_device_ids=true | all-gather | bytes 294912 | tf_op jit(solution)/shard_map/all_gather | solution.py:34
  131.9 28.0 %all-reduce.11.cloned.1.call-done = f32[256,256]{1,0:T(8,128)} async-done(((f32[256,256]{1,0:T(8,128)}), f32[256,256]{1,0:T(8,128)}) %all-reduce.11.cloned.1.call-update) | async-done | bytes 262160 | tf_op jit(solution)/shard_map/psum | solution.py:44
  159.9 0.0 all-reduce.13.cloned.1.call-update
  159.9 0.0 reduce-scatter.5.cloned.1.call-start
  160.0 1.0 fusion.18
  161.0 0.0 reduce-scatter.5.cloned.1.call-update
  161.0 54.3 %all-reduce.13.cloned.1.call-done = f32[256,256]{1,0:T(8,128)} async-done(((f32[256,256]{1,0:T(8,128)}), f32[256,256]{1,0:T(8,128)}) %all-reduce.13.cloned.1.call-update) | async-done | bytes 262160 | tf_op jit(solution)/shard_map/psum | solution.py:44
  215.3 1.6 multiply_reduce_fusion.2
  217.6 0.0 reduce-scatter.5.cloned.1.call-done
  217.6 1.8 fusion.7
  (3 shorter events, 0.0 us)
Async XLA Ops:
  7.4 16.0 %copy-start.1 = (f32[64,256]{1,0:T(8,128)S(1)}, f32[64,256]{1,0:T(8,128)}, u32[]{:S(2)}) copy-start(f32[64,256]{1,0:T(8,128)} %param.3) | copy-start | bytes 196612
  7.4 50.3 %all-reduce.7.cloned.1.call-start = ((), (), s32[]{:S(2)}) async-start(), calls=%async_computation.2 | async-start | bytes 524288 | tf_op jit(solution)/shard_map/psum | solution.py:44
  9.5 48.2 %all-gather.2.cloned.1.call-start = ((), (), s32[]{:S(2)}) async-start(), calls=%async_computation.4 | async-start | bytes 1179648 | tf_op jit(solution)/shard_map/all_gather | solution.py:18
  10.1 102.9 %all-reduce.9.cloned.1.call-start = ((), (), s32[]{:S(2)}) async-start(), calls=%async_computation.3 | async-start | bytes 524288 | tf_op jit(solution)/shard_map/psum | solution.py:44
  57.6 57.6 %reduce-scatter.3.cloned.1.call-start = ((), (), s32[]{:S(2)}) async-start(), calls=%async_computation.5 | async-start | bytes 327680 | tf_op jit(solution)/shard_map/reduce_scatter | solution.py:35
  57.7 1.6 copy-start
  86.3 73.7 %all-reduce.11.cloned.1.call-start = ((), (), s32[]{:S(2)}) async-start(), calls=%async_computation.6 | async-start | bytes 524288 | tf_op jit(solution)/shard_map/psum | solution.py:44
  117.7 97.6 %all-reduce.13.cloned.1.call-start = ((), (), s32[]{:S(2)}) async-start(), calls=%async_computation.7 | async-start | bytes 524288 | tf_op jit(solution)/shard_map/psum | solution.py:44
  159.9 57.7 %reduce-scatter.5.cloned.1.call-start = ((), (), s32[]{:S(2)}) async-start(), calls=%async_computation.8 | async-start | bytes 327680 | tf_op jit(solution)/shard_map/reduce_scatter | solution.py:35
Sparse Core Ops, SparseCore 0:
  11.1 46.4 all-reduce.6
  86.4 21.5 reduce-scatter.2
  117.8 42.0 all-reduce.10
  163.2 24.3 reduce-scatter.4
Sparse Core Ops, SparseCore 1:
  11.6 26.0 all-gather.1
  57.7 55.2 all-reduce.8
  160.0 55.2 all-reduce.12
